TPU v7x, 32 devices: a whole 2x2x4 slice. The times are simulated.
32 devices in a mesh: sub: 16 (over z, x, core), grid: 2 (over y).
Axes of the slice: x: 2, y: 2, z: 4, core: 2. Of those that a mesh axis runs over, the one named last changes fastest.
Arguments:
- front_entries: float32 [16, 12, 128, 2, 1536], P('sub', None, None, 'grid'), as said below
- coupling_rows: bfloat16 [16, 2048, 256], P('sub', 'grid'), may hold values from -0.09375 to 0.09375
- child_map: int32 [16, 2048], P('sub'), may hold values from 0 to 3071, as said below
Outputs:
- factored: float32 [16, 12, 128, 2, 1536], P('sub', None, None, 'grid')
Inputs may be any that keep to these rules, and one draw needn't show every extreme that they name: `child_map`: rows 2 p and 2 p + 1 each hold 2048 distinct indices, and together they name every index of the parent front. `front_entries`: each front is symmetric, and stays positive definite after both children's updates are subtracted.
All inputs are finite; a program needn't handle non-finite values.
Results may differ from a plain program's by a relative error of at most 0.0003.
Values may be sent and summed in bfloat16 or wider, within the bound.
A program may use at most 128 MiB of HBM per device.

v0:
```python
import jax
import jax.numpy as jnp
from jax import lax
from jax.sharding import PartitionSpec as P

NB = 128
PF = 3072
PIV = 1024


def partner(shard, axis, apart):
    return lax.ppermute(shard, axis, [(i, i ^ 1 << apart) for i in range(lax.axis_size(axis))])


def broadcast(shard, axis, root):
    mine = lax.axis_index(axis) == root
    return lax.psum(jnp.where(mine, shard, jnp.zeros_like(shard)), axis)


def invert_map(mapping):
    return (
        jnp.full((PF,), -1, jnp.int32)
        .at[mapping]
        .set(jnp.arange(mapping.shape[0], dtype=jnp.int32))
    )


def select_rows(table, inverse, wanted):
    index = inverse[wanted]
    found = index >= 0
    picked = table[jnp.where(found, index, 0)]
    return jnp.where(found[:, None], picked, jnp.zeros((), table.dtype))


def outer_product(left, right, precision):
    return lax.dot_general(
        left,
        right,
        (((1,), (1,)), ((), ())),
        precision=precision,
        preferred_element_type=jnp.float32,
    )


def block_indices(block_ids):
    offsets = jnp.arange(NB, dtype=jnp.int32)
    return (block_ids[:, None] * NB + offsets[None, :]).reshape(-1)


def on_device(front_entries, coupling_rows, child_map):
    sibling = lax.axis_index("sub") % 2
    column_owner = lax.axis_index("grid")
    grid_count = lax.axis_size("grid")
    row_blocks = front_entries.shape[1]
    col_width = front_entries.shape[4]
    col_blocks = col_width // NB
    local = front_entries.reshape(row_blocks * NB, col_width)
    row_block_ids = jnp.arange(row_blocks, dtype=jnp.int32) * 2 + sibling
    col_block_ids = jnp.arange(col_blocks, dtype=jnp.int32) * grid_count + column_owner
    my_rows = block_indices(row_block_ids)
    my_cols = block_indices(col_block_ids)
    own_map = child_map[0]
    own_inverse = invert_map(own_map)
    everything = lax.all_gather(coupling_rows, "grid", axis=1, tiled=True)[0]
    update = outer_product(coupling_rows[0], everything, None)
    dest_blocks = (
        jnp.arange(grid_count, dtype=jnp.int32)[:, None]
        + jnp.arange(col_blocks, dtype=jnp.int32)[None, :] * grid_count
    )
    dest_cols = block_indices(dest_blocks.reshape(-1))
    col_index = own_inverse[dest_cols]
    found = col_index >= 0
    spread = jnp.where(found[None, :], update[:, jnp.where(found, col_index, 0)], 0.0)
    spread = spread.reshape(update.shape[0], grid_count, col_width)
    arrived = (
        lax.all_to_all(spread.astype(jnp.bfloat16), "grid", split_axis=1, concat_axis=0, tiled=True)
        .astype(spread.dtype)
        .reshape(-1, col_width)
    )
    partner_rows = block_indices(jnp.arange(row_blocks, dtype=jnp.int32) * 2 + (1 - sibling))
    keep = select_rows(arrived, own_inverse, my_rows)
    give = select_rows(arrived, own_inverse, partner_rows)
    received = partner(give.astype(jnp.bfloat16), "sub", 0).astype(give.dtype)
    local = local - keep - received
    highest = lax.Precision.HIGHEST
    identity = jnp.eye(NB, dtype=jnp.float32)
    col_repeat = jnp.repeat(col_block_ids, NB)
    row_repeat = jnp.repeat(row_block_ids, NB)
    for step in range(PIV // NB):
        owner = step % grid_count
        local_col = step // grid_count * NB
        first = step // 2 * NB
        column = broadcast(local[:, local_col : local_col + NB], "grid", owner)
        own_pivot = local[first : first + NB, :]
        own_diag = column[first : first + NB]
        other_pivot, other_diag = (
            partner(own_pivot.astype(jnp.bfloat16), "sub", 0).astype(own_pivot.dtype),
            partner(own_diag.astype(jnp.bfloat16), "sub", 0).astype(own_diag.dtype),
        )
        holder = sibling == step % 2
        pivot_rows = jnp.where(holder, own_pivot, other_pivot)
        diagonal = jnp.where(holder, own_diag, other_diag)
        factor = jnp.linalg.cholesky(diagonal)
        inverse = jax.scipy.linalg.solve_triangular(factor, identity, lower=True)
        left = outer_product(column, inverse, highest)
        right = lax.dot_general(
            pivot_rows,
            inverse,
            (((0,), (1,)), ((), ())),
            precision=highest,
            preferred_element_type=jnp.float32,
        )
        left_live = jnp.where((row_repeat > step)[:, None], left, 0.0)
        right_live = jnp.where((col_repeat > step)[:, None], right, 0.0)
        local = local - outer_product(left_live, right_live, highest)
        is_owner = column_owner == owner
        current = local[:, local_col : local_col + NB]
        new_col = jnp.where(is_owner, jnp.where((row_repeat >= step)[:, None], left, 0.0), current)
        local = lax.dynamic_update_slice(local, new_col, (0, local_col))
    rows_global = my_rows[:, None]
    cols_global = my_cols[None, :]
    cleared = (cols_global < PIV) & (rows_global < cols_global) | (rows_global < PIV) & (
        cols_global >= PIV
    )
    result = jnp.where(cleared, 0.0, local)
    return result.reshape(front_entries.shape)


def solution(mesh):
    return jax.shard_map(
        on_device,
        mesh=mesh,
        in_specs=(P("sub", None, None, "grid", None), P("sub", "grid", None), P("sub", None)),
        out_specs=P("sub", None, None, "grid", None),
        check_vma=False,
    )
```

profile of v0, /device:TPU:0, one launch (start us, length us, event | category | flops | bytes accessed | tf_op | source)
XLA Modules:
  0.0 928.3 jit_solution(12365081881427203168)
XLA Ops:
  16.3 17.4 %gather_fusion.1 = s32[3072]{0:T(1024)S(1)} fusion(s32[3072]{0:T(1024)S(1)} %scatter_custom_fusion, s32[3072]{0:T(1024)S(1)} %broadcast_clamp_fusion.1), kind=kCustom, calls=%fused_computation.1 | custom fusion | bytes 36864 | tf_op jit(solution)/shard_map/gather | solution.py:71
  38.2 18.6 %gather_fusion.2 = bf16[3072,1024]{1,0:T(8,128)(2,1)} fusion(bf16[1024,2048]{0,1:T(8,128)(2,1)} %fusion, s32[3072]{0:T(1024)S(1)} %broadcast_clamp_fusion), kind=kCustom, calls=%fused_computation.2 | custom fusion | bytes 12595200 | tf_op jit(solution)/shard_map/gather | solution.py:73
  79.0 62.5 %all-to-all-done = bf16[1024,2,1536]{0,2,1:T(8,128)(2,1)} async-done(((bf16[1024,2,1536]{0,2,1:T(8,128)(2,1)}), bf16[1024,2,1536]{0,2,1:T(8,128)(2,1)}, u32[]{:S(2)}, u32[]{:S(2)}) %all-to-all-start) | async-done | bytes 6291488 | tf_op jit(solution)/shard_map/all_to_all | solution.py:76
  150.3 12.6 %copy.43 = f32[2,1024,1,1536]{3,1,0,2:T(8,128)} copy(f32[2,1024,1,1536]{1,3,0,2:T(8,128)} %convert_bitcast_fusion) | data formatting | bytes 25165824 | tf_op jit(solution)/shard_map/convert_element_type | solution.py:77
  162.9 14.9 %gather_fusion.5 = bf16[1536,1536]{1,0:T(8,128)(2,1)} fusion(f32[2048,1536]{1,0:T(8,128)} %bitcast.198, s32[2048]{0:T(1024)S(1)} %pad_clamp_fusion), kind=kCustom, calls=%fused_computation.5 | custom fusion | bytes 9443328 | tf_op jit(solution)/shard_map/gather | solution.py:31
  217.7 14.9 %gather_fusion.3 = f32[1536,1536]{1,0:T(8,128)} fusion(f32[2048,1536]{1,0:T(8,128)} %bitcast.199, s32[2048]{0:T(1024)S(1)} %pad_clamp_fusion.2), kind=kCustom, calls=%fused_computation.3 | custom fusion | bytes 18880512 | tf_op jit(solution)/shard_map/gather | solution.py:31
  256.4 34.3 %all-reduce.9.cloned.1.call-done = f32[1536,128]{0,1:T(8,128)} async-done(((f32[1536,128]{0,1:T(8,128)}), f32[1536,128]{0,1:T(8,128)}) %all-reduce.9.cloned.1.call-update) | async-done | bytes 786448 | tf_op jit(solution)/shard_map/psum | solution.py:17
  294.3 11.7 %cholesky.134 = f32[128,128]{1,0:T(8,128)S(1)} custom-call(f32[128,128]{1,0:T(8,128)S(1)} %fusion.106), custom_call_target="Cholesky" | custom-call | tf_op jit(solution)/shard_map/jit(cholesky)/cholesky | solution.py:103
  321.6 11.9 %convolution_subtract_fusion.7 = f32[1536,1536]{0,1:T(8,128)} fusion(f32[1536,1536]{0,1:T(8,128)} %copy-done.3, f32[1536,128]{0,1:T(8,128)S(1)} %convolution_select_fusion.7, f32[1536,128]{0,1:T(8,128)S(1)} %fusion.125, pred[1536]{0:T(1024)(128)(4,1)S(1)} %broadcast_bitcast_fusion.23), kind=kOutput, calls=%fused_computation.16 | convolution fusion | flops 3626434560 | bytes 20448768 | tf_op jit(solution)/shard_map/dot_general | solution.py:36
  336.5 34.1 %all-reduce.11.cloned.1.call-done = f32[1536,128]{0,1:T(8,128)} async-done(((f32[1536,128]{0,1:T(8,128)}), f32[1536,128]{0,1:T(8,128)}) %all-reduce.11.cloned.1.call-update) | async-done | bytes 786448 | tf_op jit(solution)/shard_map/psum | solution.py:17
  374.1 11.7 %cholesky.145 = f32[128,128]{1,0:T(8,128)S(1)} custom-call(f32[128,128]{1,0:T(8,128)S(1)} %fusion.104), custom_call_target="Cholesky" | custom-call | tf_op jit(solution)/shard_map/jit(cholesky)/cholesky | solution.py:103
  417.6 33.8 %all-reduce.13.cloned.1.call-done = f32[1536,128]{0,1:T(8,128)} async-done(((f32[1536,128]{0,1:T(8,128)}), f32[1536,128]{0,1:T(8,128)}) %all-reduce.13.cloned.1.call-update) | async-done | bytes 786448 | tf_op jit(solution)/shard_map/psum | solution.py:17
  455.0 11.7 %cholesky.156 = f32[128,128]{1,0:T(8,128)S(1)} custom-call(f32[128,128]{1,0:T(8,128)S(1)} %fusion.102), custom_call_target="Cholesky" | custom-call | tf_op jit(solution)/shard_map/jit(cholesky)/cholesky | solution.py:103
  482.3 11.9 %convolution_subtract_fusion.5 = f32[1536,1536]{0,1:T(8,128)} fusion(f32[1536,1536]{0,1:T(8,128)} %copy-done, f32[1536,128]{0,1:T(8,128)S(1)} %convolution_select_fusion.5, f32[1536,128]{0,1:T(8,128)S(1)} %fusion.127, pred[1536]{0:T(1024)(128)(4,1)S(1)} %broadcast_bitcast_fusion.17), kind=kOutput, calls=%fused_computation.14 | convolution fusion | flops 3626434560 | bytes 20448768 | tf_op jit(solution)/shard_map/dot_general | solution.py:36
  497.1 34.1 %all-reduce.15.cloned.1.call-done = f32[1536,128]{0,1:T(8,128)} async-done(((f32[1536,128]{0,1:T(8,128)}), f32[1536,128]{0,1:T(8,128)}) %all-reduce.15.cloned.1.call-update) | async-done | bytes 786448 | tf_op jit(solution)/shard_map/psum | solution.py:17
  534.8 11.7 %cholesky.167 = f32[128,128]{1,0:T(8,128)S(1)} custom-call(f32[128,128]{1,0:T(8,128)S(1)} %fusion.100), custom_call_target="Cholesky" | custom-call | tf_op jit(solution)/shard_map/jit(cholesky)/cholesky | solution.py:103
  578.3 33.8 %all-reduce.17.cloned.1.call-done = f32[1536,128]{0,1:T(8,128)} async-done(((f32[1536,128]{0,1:T(8,128)}), f32[1536,128]{0,1:T(8,128)}) %all-reduce.17.cloned.1.call-update) | async-done | bytes 786448 | tf_op jit(solution)/shard_map/psum | solution.py:17
  615.7 11.7 %cholesky.178 = f32[128,128]{1,0:T(8,128)S(1)} custom-call(f32[128,128]{1,0:T(8,128)S(1)} %fusion.98), custom_call_target="Cholesky" | custom-call | tf_op jit(solution)/shard_map/jit(cholesky)/cholesky | solution.py:103
  642.9 11.9 %convolution_subtract_fusion.3 = f32[1536,1536]{0,1:T(8,128)} fusion(f32[1536,1536]{0,1:T(8,128)} %copy-done.1, f32[1536,128]{0,1:T(8,128)S(1)} %convolution_select_fusion.3, f32[1536,128]{0,1:T(8,128)S(1)} %fusion.129, pred[1536]{0:T(1024)(128)(4,1)S(1)} %broadcast_bitcast_fusion.11), kind=kOutput, calls=%fused_computation.12 | convolution fusion | flops 3626434560 | bytes 20448768 | tf_op jit(solution)/shard_map/dot_general | solution.py:36
  657.8 34.1 %all-reduce.19.cloned.1.call-done = f32[1536,128]{0,1:T(8,128)} async-done(((f32[1536,128]{0,1:T(8,128)}), f32[1536,128]{0,1:T(8,128)}) %all-reduce.19.cloned.1.call-update) | async-done | bytes 786448 | tf_op jit(solution)/shard_map/psum | solution.py:17
  738.8 34.0 %all-reduce.21.cloned.1.call-done = f32[1536,128]{0,1:T(8,128)} async-done(((f32[1536,128]{0,1:T(8,128)}), f32[1536,128]{0,1:T(8,128)}) %all-reduce.21.cloned.1.call-update) | async-done | bytes 786448 | tf_op jit(solution)/shard_map/psum | solution.py:17
  803.6 12.3 %convolution_subtract_fusion.1 = f32[1536,1536]{0,1:T(8,128)} fusion(f32[1536,1536]{0,1:T(8,128)} %copy-done.2, f32[1536,128]{0,1:T(8,128)S(1)} %convolution_select_fusion.1, f32[1536,128]{0,1:T(8,128)S(1)} %fusion.131, pred[1536]{0:T(1024)(128)(4,1)S(1)} %broadcast_bitcast_fusion.5), kind=kOutput, calls=%fused_computation.10 | convolution fusion | flops 3626434560 | bytes 20448768 | tf_op jit(solution)/shard_map/dot_general | solution.py:36
  818.7 34.3 %all-reduce.23.cloned.1.call-done = f32[1536,128]{0,1:T(8,128)} async-done(((f32[1536,128]{0,1:T(8,128)}), f32[1536,128]{0,1:T(8,128)}) %all-reduce.23.cloned.1.call-update) | async-done | bytes 786448 | tf_op jit(solution)/shard_map/psum | solution.py:17
  909.6 12.0 %copy.80 = f32[1,12,128,1,1536]{4,3,2,1,0:T(1,128)} copy(f32[1,12,128,1,1536]{4,2,1,3,0:T(8,128)} %bitcast.200) | data formatting | bytes 18874368 | tf_op jit(solution)/shard_map/reshape | solution.py:126
  (271 shorter events, 381.8 us)
Async XLA Ops:
  6.5 27.2 %all-gather.2.cloned.1.call-start = ((), (), s32[]{:S(2)}) async-start(), calls=%async_computation.1 | async-start | bytes 1572864 | tf_op jit(solution)/shard_map/all_gather | solution.py:64
  63.7 77.7 %all-to-all-start = ((bf16[1024,2,1536]{0,2,1:T(8,128)(2,1)}), bf16[1024,2,1536]{0,2,1:T(8,128)(2,1)}, u32[]{:S(2)}, u32[]{:S(2)}) async-start(bf16[1024,2,1536]{0,2,1:T(8,128)(2,1)} %select_convert_fusion), calls=%async_computation | async-start | bytes 12582912 | tf_op jit(solution)/shard_map/all_to_all | solution.py:76
  70.0 220.7 %all-reduce.9.cloned.1.call-start = ((), (), s32[]{:S(2)}) async-start(), calls=%async_computation.2 | async-start | bytes 1572864 | tf_op jit(solution)/shard_map/psum | solution.py:17
  189.9 52.4 %collective-permute-start = (bf16[1536,1536]{0,1:T(8,128)(2,1)}, bf16[1536,1536]{0,1:T(8,128)(2,1)}, u32[]{:S(2)}, u32[]{:S(2)}) collective-permute-start(bf16[1536,1536]{0,1:T(8,128)(2,1)} %select_convert_fusion.1), channel_id=1, source_target_pairs={{0,2},{2,0},{4,6},{6,4},{8,10},{10,8},{12,14},{14,12},{16,18},{18,... | collective-permute-start | bytes 14155784 | tf_op jit(solution)/shard_map/ppermute | solution.py:12
  255.6 115.0 %all-reduce.11.cloned.1.call-start = ((), (), s32[]{:S(2)}) async-start(), calls=%async_computation.3 | async-start | bytes 1572864 | tf_op jit(solution)/shard_map/psum | solution.py:17
  291.6 1.8 collective-permute-start.1
  292.8 26.7 %collective-permute-start.2 = (bf16[128,1536]{0,1:T(8,128)(2,1)S(1)}, bf16[128,1536]{0,1:T(8,128)(2,1)S(1)}, u32[]{:S(2)}, u32[]{:S(2)}) collective-permute-start(bf16[128,1536]{0,1:T(8,128)(2,1)S(1)} %slice.263), channel_id=1, source_target_pairs={{0,2},{2,0},{4,6},{6,4},{8,10},{10,8},{12,14},{14,12},{16,18},{18,... | collective-permute-start | bytes 1179656 | tf_op jit(solution)/shard_map/ppermute | solution.py:12
  336.0 115.5 %all-reduce.13.cloned.1.call-start = ((), (), s32[]{:S(2)}) async-start(), calls=%async_computation.4 | async-start | bytes 1572864 | tf_op jit(solution)/shard_map/psum | solution.py:17
  371.4 1.8 collective-permute-start.3
  372.6 26.7 %collective-permute-start.4 = (bf16[128,1536]{0,1:T(8,128)(2,1)S(1)}, bf16[128,1536]{0,1:T(8,128)(2,1)S(1)}, u32[]{:S(2)}, u32[]{:S(2)}) collective-permute-start(bf16[128,1536]{0,1:T(8,128)(2,1)S(1)} %slice.262), channel_id=1, source_target_pairs={{0,2},{2,0},{4,6},{6,4},{8,10},{10,8},{12,14},{14,12},{16,18},{18,... | collective-permute-start | bytes 1179656 | tf_op jit(solution)/shard_map/ppermute | solution.py:12
  416.9 114.3 %all-reduce.15.cloned.1.call-start = ((), (), s32[]{:S(2)}) async-start(), calls=%async_computation.5 | async-start | bytes 1572864 | tf_op jit(solution)/shard_map/psum | solution.py:17
  452.3 1.8 collective-permute-start.5
  453.5 26.7 %collective-permute-start.6 = (bf16[128,1536]{0,1:T(8,128)(2,1)S(1)}, bf16[128,1536]{0,1:T(8,128)(2,1)S(1)}, u32[]{:S(2)}, u32[]{:S(2)}) collective-permute-start(bf16[128,1536]{0,1:T(8,128)(2,1)S(1)} %slice.261), channel_id=1, source_target_pairs={{0,2},{2,0},{4,6},{6,4},{8,10},{10,8},{12,14},{14,12},{16,18},{18,... | collective-permute-start | bytes 1179656 | tf_op jit(solution)/shard_map/ppermute | solution.py:12
  496.7 115.4 %all-reduce.17.cloned.1.call-start = ((), (), s32[]{:S(2)}) async-start(), calls=%async_computation.6 | async-start | bytes 1572864 | tf_op jit(solution)/shard_map/psum | solution.py:17
  532.1 1.8 collective-permute-start.7
  533.3 26.7 %collective-permute-start.8 = (bf16[128,1536]{0,1:T(8,128)(2,1)S(1)}, bf16[128,1536]{0,1:T(8,128)(2,1)S(1)}, u32[]{:S(2)}, u32[]{:S(2)}) collective-permute-start(bf16[128,1536]{0,1:T(8,128)(2,1)S(1)} %slice.260), channel_id=1, source_target_pairs={{0,2},{2,0},{4,6},{6,4},{8,10},{10,8},{12,14},{14,12},{16,18},{18,... | collective-permute-start | bytes 1179656 | tf_op jit(solution)/shard_map/ppermute | solution.py:12
  577.6 114.3 %all-reduce.19.cloned.1.call-start = ((), (), s32[]{:S(2)}) async-start(), calls=%async_computation.7 | async-start | bytes 1572864 | tf_op jit(solution)/shard_map/psum | solution.py:17
  614.2 26.7 %collective-permute-start.10 = (bf16[128,1536]{0,1:T(8,128)(2,1)S(1)}, bf16[128,1536]{0,1:T(8,128)(2,1)S(1)}, u32[]{:S(2)}, u32[]{:S(2)}) collective-permute-start(bf16[128,1536]{0,1:T(8,128)(2,1)S(1)} %slice.259), channel_id=1, source_target_pairs={{0,2},{2,0},{4,6},{6,4},{8,10},{10,8},{12,14},{14,12},{16,18},{18,... | collective-permute-start | bytes 1179656 | tf_op jit(solution)/shard_map/ppermute | solution.py:12
  657.3 115.5 %all-reduce.21.cloned.1.call-start = ((), (), s32[]{:S(2)}) async-start(), calls=%async_computation.8 | async-start | bytes 1572864 | tf_op jit(solution)/shard_map/psum | solution.py:17
  694.0 26.7 %collective-permute-start.12 = (bf16[128,1536]{0,1:T(8,128)(2,1)S(1)}, bf16[128,1536]{0,1:T(8,128)(2,1)S(1)}, u32[]{:S(2)}, u32[]{:S(2)}) collective-permute-start(bf16[128,1536]{0,1:T(8,128)(2,1)S(1)} %slice.258), channel_id=1, source_target_pairs={{0,2},{2,0},{4,6},{6,4},{8,10},{10,8},{12,14},{14,12},{16,18},{18,... | collective-permute-start | bytes 1179656 | tf_op jit(solution)/shard_map/ppermute | solution.py:12
  738.3 114.7 %all-reduce.23.cloned.1.call-start = ((), (), s32[]{:S(2)}) async-start(), calls=%async_computation.9 | async-start | bytes 1572864 | tf_op jit(solution)/shard_map/psum | solution.py:17
  774.8 26.7 %collective-permute-start.14 = (bf16[128,1536]{0,1:T(8,128)(2,1)S(1)}, bf16[128,1536]{0,1:T(8,128)(2,1)S(1)}, u32[]{:S(2)}, u32[]{:S(2)}) collective-permute-start(bf16[128,1536]{0,1:T(8,128)(2,1)S(1)} %slice.257), channel_id=1, source_target_pairs={{0,2},{2,0},{4,6},{6,4},{8,10},{10,8},{12,14},{14,12},{16,18},{18,... | collective-permute-start | bytes 1179656 | tf_op jit(solution)/shard_map/ppermute | solution.py:12
  853.8 1.8 collective-permute-start.15
  855.0 26.7 %collective-permute-start.16 = (bf16[128,1536]{0,1:T(8,128)(2,1)S(1)}, bf16[128,1536]{0,1:T(8,128)(2,1)S(1)}, u32[]{:S(2)}, u32[]{:S(2)}) collective-permute-start(bf16[128,1536]{0,1:T(8,128)(2,1)S(1)} %slice.256), channel_id=1, source_target_pairs={{0,2},{2,0},{4,6},{6,4},{8,10},{10,8},{12,14},{14,12},{16,18},{18,... | collective-permute-start | bytes 1179656 | tf_op jit(solution)/shard_map/ppermute | solution.py:12
  (9 other events, 58.5 us)
Sparse Core Ops, SparseCore 0:
  8.9 23.9 all-gather.1
  255.7 34.9 all-reduce.8
  336.1 34.4 all-reduce.10
  417.0 34.3 all-reduce.12
  496.8 34.4 all-reduce.14
  577.7 34.3 all-reduce.16
  657.5 34.4 all-reduce.18
  738.4 34.3 all-reduce.20
  818.5 34.3 all-reduce.22
where the time goes:
time: 936 us; the launch traced here: 928 us
  waiting for transfers between devices  336 us (36%)
  other arithmetic  242 us (26%)
  local copies, waits for them, and re-layouts  193 us (21%)
  matrix products  129 us (14%)
  between operations  14.4 us (2%)
  starting transfers between devices  13.6 us (1%)
    psum x8, waiting for transfers between devices, broadcast(): return lax.psum(jnp.where(mine, shard, jnp.zeros_like(shard)), axis)  273 us
    dot_general x17, matrix products, outer_product(): lax.dot_general(left, right, (((1,), (1,)), ((), ())), precision=precisio...  111 us
    another operation x24, other arithmetic, on_device(): factor = jnp.linalg.cholesky(diagonal)  99.6 us
    another operation x16, other arithmetic, on_device(): inverse = jax.scipy.linalg.solve_triangular(factor, identity, lower=True)  83.6 us
    all_to_all x1, waiting for transfers between devices, on_device(): lax.all_to_all(spread.astype(jnp.bfloat16), 'grid', split_axis=1, concat_...  62.5 us
    gather x4, local copies, waits for them, and re-layouts, select_rows(): picked = table[jnp.where(found, index, 0)]  46.1 us
    unnamed x13, local copies, waits for them, and re-layouts  23.9 us
  transfers between devices with their start and end apart: 27, of which 9 were waited for; matrix products, arithmetic and copies ran while one was open for 33% of the time, Pallas kernels for 0%

commit v1 on v0

--- a/solution.py
+++ b/solution.py
@@ -8,13 +8,19 @@
 PIV = 1024
 
 
+def summed_here(x, name):
+    shards = lax.all_gather(x, name, axis=0, tiled=False)
+    acc = shards.sum(axis=0)
+    return acc
+
+
 def partner(shard, axis, apart):
     return lax.ppermute(shard, axis, [(i, i ^ 1 << apart) for i in range(lax.axis_size(axis))])
 
 
 def broadcast(shard, axis, root):
     mine = lax.axis_index(axis) == root
-    return lax.psum(jnp.where(mine, shard, jnp.zeros_like(shard)), axis)
+    return summed_here(jnp.where(mine, shard, jnp.zeros_like(shard)), axis)
 
 
 def invert_map(mapping):

time: 936 us -> 836 us (0.89)
  waiting for transfers between devices: 336 us -> 279 us
  local copies, waits for them, and re-layouts: 193 us -> 151 us
    psum x8 -> x0, waiting for transfers between devices: 273 us -> none  [broadcast(): return lax.psum(jnp.where(mine, shard, jnp.zeros_like(shard)), axis)]
    all_gather x0 -> x8, waiting for transfers between devices: none -> 215 us  [summed_here(): shards = lax.all_gather(x, name, axis=0, tiled=False)]
    gather x4 -> x2, local copies, waits for them, and re-layouts: 46.1 us -> 29.9 us  [select_rows(): picked = table[jnp.where(found, index, 0)]]
    reduce_sum x0 -> x8, other arithmetic: none -> 12.7 us  [summed_here(): acc = shards.sum(axis=0)]
    select_n x1 -> x0, local copies, waits for them, and re-layouts: 9.63 us -> none  [on_device(): result = jnp.where(cleared, 0.0, local)]
    reshape x1 -> x0, local copies, waits for them, and re-layouts: 9.61 us -> none  [on_device(): local = front_entries.reshape(row_blocks * NB, col_width)]
    unnamed x13 -> x19, local copies, waits for them, and re-layouts: 23.9 us -> 24.6 us
where the time goes in v1:
time: 836 us; the launch traced here: 830 us
  waiting for transfers between devices  279 us (33%)
  other arithmetic  247 us (30%)
  local copies, waits for them, and re-layouts  151 us (18%)
  matrix products  125 us (15%)
  between operations  14.7 us (2%)
  starting transfers between devices  14.1 us (2%)
    all_gather x8, waiting for transfers between devices, summed_here(): shards = lax.all_gather(x, name, axis=0, tiled=False)  215 us
    dot_general x17, matrix products, outer_product(): lax.dot_general(left, right, (((1,), (1,)), ((), ())), precision=precisio...  102 us
    another operation x24, other arithmetic, on_device(): factor = jnp.linalg.cholesky(diagonal)  99.7 us
    another operation x16, other arithmetic, on_device(): inverse = jax.scipy.linalg.solve_triangular(factor, identity, lower=True)  84.1 us
    all_to_all x1, waiting for transfers between devices, on_device(): lax.all_to_all(spread.astype(jnp.bfloat16), 'grid', split_axis=1, concat_...  62.5 us
    gather x2, local copies, waits for them, and re-layouts, select_rows(): picked = table[jnp.where(found, index, 0)]  29.9 us
    unnamed x19, local copies, waits for them, and re-layouts  24.6 us
    dot_general x8, matrix products, on_device(): lax.dot_general(pivot_rows, inverse, (((0,), (1,)), ((), ())), precision=...  21.2 us
  transfers between devices with their start and end apart: 27, of which 9 were waited for; matrix products, arithmetic and copies ran while one was open for 33% of the time, Pallas kernels for 0%

profile of v1, /device:TPU:0, one launch (start us, length us, event | category | flops | bytes accessed | tf_op | source)
XLA Modules:
  0.0 830.4 jit_solution(10001268191058713503)
XLA Ops:
  16.3 17.4 %gather_fusion.1 = s32[3072]{0:T(1024)S(1)} fusion(s32[3072]{0:T(1024)S(1)} %scatter_custom_fusion, s32[3072]{0:T(1024)S(1)} %broadcast_clamp_fusion.1), kind=kCustom, calls=%fused_computation.1 | custom fusion | bytes 36864 | tf_op jit(solution)/shard_map/gather | solution.py:77
  38.2 18.6 %gather_fusion.2 = bf16[3072,1024]{1,0:T(8,128)(2,1)} fusion(bf16[1024,2048]{0,1:T(8,128)(2,1)} %fusion.1, s32[3072]{0:T(1024)S(1)} %broadcast_clamp_fusion), kind=kCustom, calls=%fused_computation.2 | custom fusion | bytes 12595200 | tf_op jit(solution)/shard_map/gather | solution.py:79
  79.0 62.5 %all-to-all-done = bf16[1024,2,1536]{0,2,1:T(8,128)(2,1)} async-done(((bf16[1024,2,1536]{0,2,1:T(8,128)(2,1)}), bf16[1024,2,1536]{0,2,1:T(8,128)(2,1)}, u32[]{:S(2)}, u32[]{:S(2)}) %all-to-all-start) | async-done | bytes 6291488 | tf_op jit(solution)/shard_map/all_to_all | solution.py:82
  150.3 12.6 %copy.27 = f32[2,1024,1,1536]{3,1,0,2:T(8,128)} copy(f32[2,1024,1,1536]{1,3,0,2:T(8,128)} %convert_bitcast_fusion) | data formatting | bytes 25165824 | tf_op jit(solution)/shard_map/convert_element_type | solution.py:83
  162.9 14.9 %gather_fusion.5 = bf16[1536,1536]{1,0:T(8,128)(2,1)} fusion(f32[2048,1536]{1,0:T(8,128)} %bitcast.209, s32[2048]{0:T(1024)S(1)} %pad_clamp_fusion), kind=kCustom, calls=%fused_computation.5 | custom fusion | bytes 9443328 | tf_op jit(solution)/shard_map/gather | solution.py:37
  200.7 14.9 %gather_fusion.3 = f32[1536,1536]{1,0:T(8,128)} fusion(f32[2048,1536]{1,0:T(8,128)} %bitcast.210, s32[2048]{0:T(1024)S(1)} %pad_clamp_fusion.2), kind=kCustom, calls=%fused_computation.3 | custom fusion | bytes 18880512 | tf_op jit(solution)/shard_map/gather | solution.py:37
  229.9 27.2 %all-gather.20.cloned.1.call-done = f32[3072,128]{1,0:T(8,128)} async-done(((f32[1536,128]{1,0:T(8,128)}), f32[3072,128]{1,0:T(8,128)}) %all-gather.20.cloned.1.call-update) | async-done | bytes 1572880 | tf_op jit(solution)/shard_map/all_gather | solution.py:12
  260.8 11.7 %cholesky.134 = f32[128,128]{1,0:T(8,128)S(1)} custom-call(f32[128,128]{1,0:T(8,128)S(1)} %fusion.107), custom_call_target="Cholesky" | custom-call | tf_op jit(solution)/shard_map/jit(cholesky)/cholesky | solution.py:109
  287.6 11.9 %convolution_subtract_fusion.7 = f32[1536,1536]{1,0:T(8,128)} fusion(f32[1536,1536]{1,0:T(8,128)} %copy-done.3, f32[1536,128]{1,0:T(8,128)S(1)} %convolution_select_fusion.7, f32[1536,128]{1,0:T(8,128)S(1)} %fusion.126, pred[1536]{0:T(1024)(128)(4,1)S(1)} %broadcast_bitcast_fusion.23), kind=kOutput, calls=%fused_computation.16 | convolution fusion | flops 3626434560 | bytes 20448768 | tf_op jit(solution)/shard_map/dot_general | solution.py:42
  302.5 26.9 %all-gather.22.cloned.1.call-done = f32[3072,128]{1,0:T(8,128)} async-done(((f32[1536,128]{1,0:T(8,128)}), f32[3072,128]{1,0:T(8,128)}) %all-gather.22.cloned.1.call-update) | async-done | bytes 1572880 | tf_op jit(solution)/shard_map/all_gather | solution.py:12
  333.1 11.7 %cholesky.145 = f32[128,128]{1,0:T(8,128)S(1)} custom-call(f32[128,128]{1,0:T(8,128)S(1)} %fusion.105), custom_call_target="Cholesky" | custom-call | tf_op jit(solution)/shard_map/jit(cholesky)/cholesky | solution.py:109
  376.4 26.7 %all-gather.24.cloned.1.call-done = f32[3072,128]{1,0:T(8,128)} async-done(((f32[1536,128]{1,0:T(8,128)}), f32[3072,128]{1,0:T(8,128)}) %all-gather.24.cloned.1.call-update) | async-done | bytes 1572880 | tf_op jit(solution)/shard_map/all_gather | solution.py:12
  406.9 11.7 %cholesky.156 = f32[128,128]{1,0:T(8,128)S(1)} custom-call(f32[128,128]{1,0:T(8,128)S(1)} %fusion.103), custom_call_target="Cholesky" | custom-call | tf_op jit(solution)/shard_map/jit(cholesky)/cholesky | solution.py:109
  433.6 11.9 %convolution_subtract_fusion.5 = f32[1536,1536]{1,0:T(8,128)} fusion(f32[1536,1536]{1,0:T(8,128)} %copy-done, f32[1536,128]{1,0:T(8,128)S(1)} %convolution_select_fusion.5, f32[1536,128]{1,0:T(8,128)S(1)} %fusion.128, pred[1536]{0:T(1024)(128)(4,1)S(1)} %broadcast_bitcast_fusion.17), kind=kOutput, calls=%fused_computation.14 | convolution fusion | flops 3626434560 | bytes 20448768 | tf_op jit(solution)/shard_map/dot_general | solution.py:42
  448.5 26.9 %all-gather.26.cloned.1.call-done = f32[3072,128]{1,0:T(8,128)} async-done(((f32[1536,128]{1,0:T(8,128)}), f32[3072,128]{1,0:T(8,128)}) %all-gather.26.cloned.1.call-update) | async-done | bytes 1572880 | tf_op jit(solution)/shard_map/all_gather | solution.py:12
  479.2 11.7 %cholesky.167 = f32[128,128]{1,0:T(8,128)S(1)} custom-call(f32[128,128]{1,0:T(8,128)S(1)} %fusion.101), custom_call_target="Cholesky" | custom-call | tf_op jit(solution)/shard_map/jit(cholesky)/cholesky | solution.py:109
  522.5 26.7 %all-gather.28.cloned.1.call-done = f32[3072,128]{1,0:T(8,128)} async-done(((f32[1536,128]{1,0:T(8,128)}), f32[3072,128]{1,0:T(8,128)}) %all-gather.28.cloned.1.call-update) | async-done | bytes 1572880 | tf_op jit(solution)/shard_map/all_gather | solution.py:12
  552.9 11.7 %cholesky.178 = f32[128,128]{1,0:T(8,128)S(1)} custom-call(f32[128,128]{1,0:T(8,128)S(1)} %fusion.99), custom_call_target="Cholesky" | custom-call | tf_op jit(solution)/shard_map/jit(cholesky)/cholesky | solution.py:109
  579.7 11.9 %convolution_subtract_fusion.3 = f32[1536,1536]{1,0:T(8,128)} fusion(f32[1536,1536]{1,0:T(8,128)} %copy-done.1, f32[1536,128]{1,0:T(8,128)S(1)} %convolution_select_fusion.3, f32[1536,128]{1,0:T(8,128)S(1)} %fusion.130, pred[1536]{0:T(1024)(128)(4,1)S(1)} %broadcast_bitcast_fusion.11), kind=kOutput, calls=%fused_computation.12 | convolution fusion | flops 3626434560 | bytes 20448768 | tf_op jit(solution)/shard_map/dot_general | solution.py:42
  594.6 26.9 %all-gather.30.cloned.1.call-done = f32[3072,128]{1,0:T(8,128)} async-done(((f32[1536,128]{1,0:T(8,128)}), f32[3072,128]{1,0:T(8,128)}) %all-gather.30.cloned.1.call-update) | async-done | bytes 1572880 | tf_op jit(solution)/shard_map/all_gather | solution.py:12
  625.2 11.7 %cholesky.189 = f32[128,128]{1,0:T(8,128)S(1)} custom-call(f32[128,128]{1,0:T(8,128)S(1)} %fusion.97), custom_call_target="Cholesky" | custom-call | tf_op jit(solution)/shard_map/jit(cholesky)/cholesky | solution.py:109
  668.3 26.9 %all-gather.32.cloned.1.call-done = f32[3072,128]{1,0:T(8,128)} async-done(((f32[1536,128]{1,0:T(8,128)}), f32[3072,128]{1,0:T(8,128)}) %all-gather.32.cloned.1.call-update) | async-done | bytes 1572880 | tf_op jit(solution)/shard_map/all_gather | solution.py:12
  725.7 12.3 %convolution_subtract_fusion.1 = f32[1536,1536]{1,0:T(8,128)} fusion(f32[1536,1536]{1,0:T(8,128)} %copy-done.2, f32[1536,128]{1,0:T(8,128)S(1)} %convolution_select_fusion.1, f32[1536,128]{1,0:T(8,128)S(1)} %fusion.132, pred[1536]{0:T(1024)(128)(4,1)S(1)} %broadcast_bitcast_fusion.5), kind=kOutput, calls=%fused_computation.10 | convolution fusion | flops 3626434560 | bytes 20448768 | tf_op jit(solution)/shard_map/dot_general | solution.py:42
  741.0 26.9 %all-gather.34.cloned.1.call-done = f32[3072,128]{1,0:T(8,128)} async-done(((f32[1536,128]{1,0:T(8,128)}), f32[3072,128]{1,0:T(8,128)}) %all-gather.34.cloned.1.call-update) | async-done | bytes 1572880 | tf_op jit(solution)/shard_map/all_gather | solution.py:12
  (285 shorter events, 341.3 us)
Async XLA Ops:
  6.5 27.2 %all-gather.18.cloned.1.call-start = ((), (), s32[]{:S(2)}) async-start(), calls=%async_computation.1 | async-start | bytes 1572864 | tf_op jit(solution)/shard_map/all_gather | solution.py:70
  63.7 77.7 %all-to-all-start = ((bf16[1024,2,1536]{0,2,1:T(8,128)(2,1)}), bf16[1024,2,1536]{0,2,1:T(8,128)(2,1)}, u32[]{:S(2)}, u32[]{:S(2)}) async-start(bf16[1024,2,1536]{0,2,1:T(8,128)(2,1)} %select_convert_fusion), calls=%async_computation | async-start | bytes 12582912 | tf_op jit(solution)/shard_map/all_to_all | solution.py:82
  70.0 187.0 %all-gather.20.cloned.1.call-start = ((), (), s32[]{:S(2)}) async-start(), calls=%async_computation.2 | async-start | bytes 2359296 | tf_op jit(solution)/shard_map/all_gather | solution.py:12
  183.2 32.5 %collective-permute-start = (bf16[1536,1536]{1,0:T(8,128)(2,1)}, bf16[1536,1536]{1,0:T(8,128)(2,1)}, u32[]{:S(2)}, u32[]{:S(2)}) collective-permute-start(bf16[1536,1536]{1,0:T(8,128)(2,1)} %select_convert_fusion.1), channel_id=1, source_target_pairs={{0,2},{2,0},{4,6},{6,4},{8,10},{10,8},{12,14},{14,12},{16,18},{18,... | collective-permute-start | bytes 14155784 | tf_op jit(solution)/shard_map/ppermute | solution.py:18
  229.1 100.3 %all-gather.22.cloned.1.call-start = ((), (), s32[]{:S(2)}) async-start(), calls=%async_computation.3 | async-start | bytes 2359296 | tf_op jit(solution)/shard_map/all_gather | solution.py:12
  258.8 1.9 collective-permute-start.1
  260.1 24.8 %collective-permute-start.2 = (bf16[128,1536]{1,0:T(8,128)(2,1)S(1)}, bf16[128,1536]{1,0:T(8,128)(2,1)S(1)}, u32[]{:S(2)}, u32[]{:S(2)}) collective-permute-start(bf16[128,1536]{1,0:T(8,128)(2,1)S(1)} %slice.247), channel_id=1, source_target_pairs={{0,2},{2,0},{4,6},{6,4},{8,10},{10,8},{12,14},{14,12},{16,18},{18,... | collective-permute-start | bytes 1179656 | tf_op jit(solution)/shard_map/ppermute | solution.py:18
  302.1 101.1 %all-gather.24.cloned.1.call-start = ((), (), s32[]{:S(2)}) async-start(), calls=%async_computation.4 | async-start | bytes 2359296 | tf_op jit(solution)/shard_map/all_gather | solution.py:12
  332.4 24.8 %collective-permute-start.4 = (bf16[128,1536]{1,0:T(8,128)(2,1)S(1)}, bf16[128,1536]{1,0:T(8,128)(2,1)S(1)}, u32[]{:S(2)}, u32[]{:S(2)}) collective-permute-start(bf16[128,1536]{1,0:T(8,128)(2,1)S(1)} %slice.246), channel_id=1, source_target_pairs={{0,2},{2,0},{4,6},{6,4},{8,10},{10,8},{12,14},{14,12},{16,18},{18,... | collective-permute-start | bytes 1179656 | tf_op jit(solution)/shard_map/ppermute | solution.py:18
  375.8 99.7 %all-gather.26.cloned.1.call-start = ((), (), s32[]{:S(2)}) async-start(), calls=%async_computation.5 | async-start | bytes 2359296 | tf_op jit(solution)/shard_map/all_gather | solution.py:12
  404.8 1.9 collective-permute-start.5
  406.2 24.8 %collective-permute-start.6 = (bf16[128,1536]{1,0:T(8,128)(2,1)S(1)}, bf16[128,1536]{1,0:T(8,128)(2,1)S(1)}, u32[]{:S(2)}, u32[]{:S(2)}) collective-permute-start(bf16[128,1536]{1,0:T(8,128)(2,1)S(1)} %slice.245), channel_id=1, source_target_pairs={{0,2},{2,0},{4,6},{6,4},{8,10},{10,8},{12,14},{14,12},{16,18},{18,... | collective-permute-start | bytes 1179656 | tf_op jit(solution)/shard_map/ppermute | solution.py:18
  448.1 101.1 %all-gather.28.cloned.1.call-start = ((), (), s32[]{:S(2)}) async-start(), calls=%async_computation.6 | async-start | bytes 2359296 | tf_op jit(solution)/shard_map/all_gather | solution.py:12
  478.5 24.8 %collective-permute-start.8 = (bf16[128,1536]{1,0:T(8,128)(2,1)S(1)}, bf16[128,1536]{1,0:T(8,128)(2,1)S(1)}, u32[]{:S(2)}, u32[]{:S(2)}) collective-permute-start(bf16[128,1536]{1,0:T(8,128)(2,1)S(1)} %slice.244), channel_id=1, source_target_pairs={{0,2},{2,0},{4,6},{6,4},{8,10},{10,8},{12,14},{14,12},{16,18},{18,... | collective-permute-start | bytes 1179656 | tf_op jit(solution)/shard_map/ppermute | solution.py:18
  521.8 99.6 %all-gather.30.cloned.1.call-start = ((), (), s32[]{:S(2)}) async-start(), calls=%async_computation.7 | async-start | bytes 2359296 | tf_op jit(solution)/shard_map/all_gather | solution.py:12
  550.9 1.9 collective-permute-start.9
  552.2 24.8 %collective-permute-start.10 = (bf16[128,1536]{1,0:T(8,128)(2,1)S(1)}, bf16[128,1536]{1,0:T(8,128)(2,1)S(1)}, u32[]{:S(2)}, u32[]{:S(2)}) collective-permute-start(bf16[128,1536]{1,0:T(8,128)(2,1)S(1)} %slice.243), channel_id=1, source_target_pairs={{0,2},{2,0},{4,6},{6,4},{8,10},{10,8},{12,14},{14,12},{16,18},{18,... | collective-permute-start | bytes 1179656 | tf_op jit(solution)/shard_map/ppermute | solution.py:18
  594.2 101.1 %all-gather.32.cloned.1.call-start = ((), (), s32[]{:S(2)}) async-start(), calls=%async_computation.8 | async-start | bytes 2359296 | tf_op jit(solution)/shard_map/all_gather | solution.py:12
  623.2 1.9 collective-permute-start.11
  624.5 24.8 %collective-permute-start.12 = (bf16[128,1536]{1,0:T(8,128)(2,1)S(1)}, bf16[128,1536]{1,0:T(8,128)(2,1)S(1)}, u32[]{:S(2)}, u32[]{:S(2)}) collective-permute-start(bf16[128,1536]{1,0:T(8,128)(2,1)S(1)} %slice.242), channel_id=1, source_target_pairs={{0,2},{2,0},{4,6},{6,4},{8,10},{10,8},{12,14},{14,12},{16,18},{18,... | collective-permute-start | bytes 1179656 | tf_op jit(solution)/shard_map/ppermute | solution.py:18
  667.9 100.0 %all-gather.34.cloned.1.call-start = ((), (), s32[]{:S(2)}) async-start(), calls=%async_computation.9 | async-start | bytes 2359296 | tf_op jit(solution)/shard_map/all_gather | solution.py:12
  698.3 24.8 %collective-permute-start.14 = (bf16[128,1536]{1,0:T(8,128)(2,1)S(1)}, bf16[128,1536]{1,0:T(8,128)(2,1)S(1)}, u32[]{:S(2)}, u32[]{:S(2)}) collective-permute-start(bf16[128,1536]{1,0:T(8,128)(2,1)S(1)} %slice.241), channel_id=1, source_target_pairs={{0,2},{2,0},{4,6},{6,4},{8,10},{10,8},{12,14},{14,12},{16,18},{18,... | collective-permute-start | bytes 1179656 | tf_op jit(solution)/shard_map/ppermute | solution.py:18
  769.7 1.9 collective-permute-start.15
  771.0 24.8 %collective-permute-start.16 = (bf16[128,1536]{1,0:T(8,128)(2,1)S(1)}, bf16[128,1536]{1,0:T(8,128)(2,1)S(1)}, u32[]{:S(2)}, u32[]{:S(2)}) collective-permute-start(bf16[128,1536]{1,0:T(8,128)(2,1)S(1)} %slice.240), channel_id=1, source_target_pairs={{0,2},{2,0},{4,6},{6,4},{8,10},{10,8},{12,14},{14,12},{16,18},{18,... | collective-permute-start | bytes 1179656 | tf_op jit(solution)/shard_map/ppermute | solution.py:18
  (8 other events, 47.9 us)
Sparse Core Ops, SparseCore 0:
  8.9 23.9 all-gather.17
  229.2 27.8 all-gather.19
  302.2 27.1 all-gather.21
  375.9 27.1 all-gather.23
  448.2 27.1 all-gather.25
  522.0 27.1 all-gather.27
  594.3 27.1 all-gather.29
  668.0 27.1 all-gather.31
  740.7 27.1 all-gather.33
